TPU v7x, 256 devices: a whole 4x4x8 slice. The times are simulated.
256 devices in a mesh: grp: 4 (over y), dev: 64 (over z, x, core).
Axes of the slice: x: 4, y: 4, z: 8, core: 2. Of those that a mesh axis runs over, the one named last changes fastest.
Arguments:
- leaf_inverse: float32 [196608, 768], P(('grp', 'dev')), as said below
- leaf_basis: float32 [196608, 256], P(('grp', 'dev')), may hold values from -0.3125 to 0.3125
- node_block: float32 [524288, 256], P(('grp', 'dev')), as said below
- node_link: float32 [524288, 256], P(('grp', 'dev')), as said below
- loads: float32 [196608, 128], P(('grp', 'dev')), may hold values from -6 to 6
- order: int32 [256, 768], P(('grp', 'dev')), may hold values from 0 to 767, each once within a row
Outputs:
- solution: float32 [196608, 128], P(('grp', 'dev'))
Inputs may be any that keep to these rules, and one draw needn't show every extreme that they name: `leaf_inverse`: each leaf's block is symmetric with a positive diagonal plus a positive semidefinite part. `node_block`: each block is symmetric with a positive diagonal plus a positive semidefinite part; leaves below the same node of level k hold equal blocks for level k. `node_link`: leaves below the same node of level k hold equal blocks for level k. `order`: each row is a permutation of 0 to 767.
All inputs are finite; a program needn't handle non-finite values.
Results may differ from a plain program's by a relative error of at most 0.0001.
Values sent between devices are 32-bit elements; how exact they have to be, the bound alone decides.
A program may use at most 128 MiB of HBM per device.

v0:
```python
import jax
import jax.numpy as jnp
from jax import lax
from jax.sharding import PartitionSpec as P


def from_partner(block, axis, apart):
    count = lax.axis_size(axis)
    route = []
    for low in range(count):
        high = low | 1 << apart
        if high != low and high < count:
            route += [(low, high), (high, low)]
    return lax.ppermute(block, axis, route)


def level_sign(level):
    return -1.0 if level % 2 else 1.0


def node_update(from_left, from_right, block, link, sign):
    width = block.shape[0]
    factor = block + from_left[:, :width] + from_right[:, :width]
    target = -sign * (from_left[:, width:] + from_right[:, width:])
    lower = jnp.linalg.cholesky(factor)
    solved = jax.scipy.linalg.cho_solve((lower, True), jnp.concatenate([link, target], axis=1))
    lifted_rows = jnp.dot(link.T, solved, precision=lax.Precision.HIGHEST)
    return (solved, lifted_rows)


def pair_sides(upward, partner, index_value, bit):
    is_left = index_value // 2**bit % 2 == 0
    from_left = jnp.where(is_left, upward, partner)
    from_right = jnp.where(is_left, partner, upward)
    return (from_left, from_right)


def shards(leaf_inverse, leaf_basis, node_block, node_link, loads, order):
    topmost_level = lax.Precision.HIGHEST
    width = node_block.shape[1]
    levels = node_block.shape[0] // width
    dev_count = lax.axis_size("dev")
    grp_count = lax.axis_size("grp")
    inner_levels = dev_count.bit_length() - 1
    outer_levels = grp_count.bit_length() - 1
    local_index = lax.axis_index("dev")
    group_index = lax.axis_index("grp")
    blocks = node_block.reshape(levels, width, width)
    links = node_link.reshape(levels, width, width)
    perm_row = order[0]
    rows = jnp.take(loads, perm_row, axis=0)
    leaf_solution = jnp.dot(
        leaf_inverse, jnp.concatenate([leaf_basis, rows], axis=1), precision=topmost_level
    )
    upward = jnp.dot(leaf_basis.T, leaf_solution, precision=topmost_level)
    stored = []
    for level in range(1, inner_levels + 1):
        partner = from_partner(upward, "dev", level - 1)
        from_left, from_right = pair_sides(upward, partner, local_index, level - 1)
        solved, upward = node_update(
            from_left, from_right, blocks[level - 1], links[level - 1], level_sign(level)
        )
        stored.append(solved)
    for step in range(1, outer_levels + 1):
        level = inner_levels + step
        partner = from_partner(upward, "grp", step - 1)
        from_left, from_right = pair_sides(upward, partner, group_index, step - 1)
        solved, upward = node_update(
            from_left, from_right, blocks[level - 1], links[level - 1], level_sign(level)
        )
        stored.append(solved)
    value = stored[-1][:, width:]
    for level in range(levels, 1, -1):
        solved = stored[level - 2]
        value = solved[:, width:] - level_sign(level - 1) * jnp.dot(
            solved[:, :width], value, precision=topmost_level
        )
    local_part = leaf_solution[:, width:] - jnp.dot(
        leaf_solution[:, :width], value, precision=topmost_level
    )
    solution = jnp.zeros_like(local_part).at[perm_row].set(local_part)
    return solution


def solution(mesh):
    in_specs = (
        P(("grp", "dev"), None),
        P(("grp", "dev"), None),
        P(("grp", "dev"), None),
        P(("grp", "dev"), None),
        P(("grp", "dev"), None),
        P(("grp", "dev"), None),
    )
    out_specs = P(("grp", "dev"), None)
    return jax.shard_map(shards, mesh=mesh, in_specs=in_specs, out_specs=out_specs, check_vma=False)
```

profile of v0, /device:TPU:1, one launch (start us, length us, event | category | flops | bytes accessed | tf_op | source)
XLA Modules:
  0.0 929.3 jit_solution(6450416014444093283)
XLA Ops:
  34.5 13.2 %cholesky.382 = f32[128,128]{1,0:T(8,128)} custom-call(f32[128,128]{1,0:T(8,128)} %cholesky.650), custom_call_target="Cholesky" | custom-call | tf_op jit(solution)/shard_map/jit(cholesky)/cholesky | solution.py:25
  50.7 11.3 %custom-call.27 = f32[1,128,128]{1,2,0:T(8,128)} custom-call(f32[1,128,128]{2,1,0:T(8,128)} %get-tuple-element.208), custom_call_target="InvertDiagBlocksLowerTriangular" | custom-call | tf_op jit(solution)/shard_map/jit(cholesky)/cholesky | solution.py:25
  65.4 13.2 %cholesky.399 = f32[128,128]{1,0:T(8,128)} custom-call(f32[128,128]{1,0:T(8,128)} %convolution_subtract_fusion.27), custom_call_target="Cholesky" | custom-call | tf_op jit(solution)/shard_map/jit(cholesky)/cholesky | solution.py:25
  91.8 21.1 %custom-call.28 = f32[2,128,128]{1,2,0:T(8,128)} custom-call(f32[2,128,128]{2,1,0:T(8,128)} %get-tuple-element.57), custom_call_target="InvertDiagBlocksLowerTriangular" | custom-call | tf_op jit(solution)/shard_map/jit(_cho_solve)/triangular_solve | solution.py:26
  148.1 13.2 %cholesky.416 = f32[128,128]{1,0:T(8,128)} custom-call(f32[128,128]{1,0:T(8,128)} %cholesky.653), custom_call_target="Cholesky" | custom-call | tf_op jit(solution)/shard_map/jit(cholesky)/cholesky | solution.py:25
  164.3 11.3 %custom-call.29 = f32[1,128,128]{1,2,0:T(8,128)} custom-call(f32[1,128,128]{2,1,0:T(8,128)} %get-tuple-element.204), custom_call_target="InvertDiagBlocksLowerTriangular" | custom-call | tf_op jit(solution)/shard_map/jit(cholesky)/cholesky | solution.py:25
  179.0 13.2 %cholesky.433 = f32[128,128]{1,0:T(8,128)} custom-call(f32[128,128]{1,0:T(8,128)} %convolution_subtract_fusion.26), custom_call_target="Cholesky" | custom-call | tf_op jit(solution)/shard_map/jit(cholesky)/cholesky | solution.py:25
  205.7 21.1 %custom-call.30 = f32[2,128,128]{1,2,0:T(8,128)} custom-call(f32[2,128,128]{2,1,0:T(8,128)} %get-tuple-element.58), custom_call_target="InvertDiagBlocksLowerTriangular" | custom-call | tf_op jit(solution)/shard_map/jit(_cho_solve)/triangular_solve | solution.py:26
  258.0 13.2 %cholesky.450 = f32[128,128]{1,0:T(8,128)} custom-call(f32[128,128]{1,0:T(8,128)} %cholesky.656), custom_call_target="Cholesky" | custom-call | tf_op jit(solution)/shard_map/jit(cholesky)/cholesky | solution.py:25
  274.2 11.3 %custom-call.31 = f32[1,128,128]{1,2,0:T(8,128)} custom-call(f32[1,128,128]{2,1,0:T(8,128)} %get-tuple-element.200), custom_call_target="InvertDiagBlocksLowerTriangular" | custom-call | tf_op jit(solution)/shard_map/jit(cholesky)/cholesky | solution.py:25
  288.9 13.2 %cholesky.467 = f32[128,128]{1,0:T(8,128)} custom-call(f32[128,128]{1,0:T(8,128)} %convolution_subtract_fusion.25), custom_call_target="Cholesky" | custom-call | tf_op jit(solution)/shard_map/jit(cholesky)/cholesky | solution.py:25
  315.9 21.1 %custom-call.32 = f32[2,128,128]{1,2,0:T(8,128)} custom-call(f32[2,128,128]{2,1,0:T(8,128)} %get-tuple-element.59), custom_call_target="InvertDiagBlocksLowerTriangular" | custom-call | tf_op jit(solution)/shard_map/jit(_cho_solve)/triangular_solve | solution.py:26
  370.4 13.2 %cholesky.484 = f32[128,128]{1,0:T(8,128)} custom-call(f32[128,128]{1,0:T(8,128)} %cholesky.659), custom_call_target="Cholesky" | custom-call | tf_op jit(solution)/shard_map/jit(cholesky)/cholesky | solution.py:25
  386.6 11.3 %custom-call.33 = f32[1,128,128]{1,2,0:T(8,128)} custom-call(f32[1,128,128]{2,1,0:T(8,128)} %get-tuple-element.196), custom_call_target="InvertDiagBlocksLowerTriangular" | custom-call | tf_op jit(solution)/shard_map/jit(cholesky)/cholesky | solution.py:25
  401.3 13.2 %cholesky.501 = f32[128,128]{1,0:T(8,128)} custom-call(f32[128,128]{1,0:T(8,128)} %convolution_subtract_fusion.24), custom_call_target="Cholesky" | custom-call | tf_op jit(solution)/shard_map/jit(cholesky)/cholesky | solution.py:25
  428.0 21.1 %custom-call.34 = f32[2,128,128]{1,2,0:T(8,128)} custom-call(f32[2,128,128]{2,1,0:T(8,128)} %get-tuple-element.60), custom_call_target="InvertDiagBlocksLowerTriangular" | custom-call | tf_op jit(solution)/shard_map/jit(_cho_solve)/triangular_solve | solution.py:26
  461.8 17.0 %collective-permute-done.4 = f32[256,384]{0,1:T(8,128)} collective-permute-done((f32[256,384]{0,1:T(8,128)}, f32[256,384]{0,1:T(8,128)}, u32[]{:S(2)}, u32[]{:S(2)}) %collective-permute-start.4) | collective-permute-done | bytes 393248 | tf_op jit(solution)/shard_map/ppermute | solution.py:14
  489.1 13.2 %cholesky.518 = f32[128,128]{1,0:T(8,128)} custom-call(f32[128,128]{1,0:T(8,128)} %cholesky.662), custom_call_target="Cholesky" | custom-call | tf_op jit(solution)/shard_map/jit(cholesky)/cholesky | solution.py:25
  505.3 11.3 %custom-call.35 = f32[1,128,128]{1,2,0:T(8,128)} custom-call(f32[1,128,128]{2,1,0:T(8,128)} %get-tuple-element.192), custom_call_target="InvertDiagBlocksLowerTriangular" | custom-call | tf_op jit(solution)/shard_map/jit(cholesky)/cholesky | solution.py:25
  520.0 13.2 %cholesky.535 = f32[128,128]{1,0:T(8,128)} custom-call(f32[128,128]{1,0:T(8,128)} %convolution_subtract_fusion.23), custom_call_target="Cholesky" | custom-call | tf_op jit(solution)/shard_map/jit(cholesky)/cholesky | solution.py:25
  546.3 21.1 %custom-call.36 = f32[2,128,128]{1,2,0:T(8,128)} custom-call(f32[2,128,128]{2,1,0:T(8,128)} %get-tuple-element.61), custom_call_target="InvertDiagBlocksLowerTriangular" | custom-call | tf_op jit(solution)/shard_map/jit(_cho_solve)/triangular_solve | solution.py:26
  588.0 15.8 %collective-permute-done.5 = f32[256,384]{0,1:T(8,128)} collective-permute-done((f32[256,384]{0,1:T(8,128)}, f32[256,384]{0,1:T(8,128)}, u32[]{:S(2)}, u32[]{:S(2)}) %collective-permute-start.5) | collective-permute-done | bytes 393248 | tf_op jit(solution)/shard_map/ppermute | solution.py:14
  614.1 13.2 %cholesky.552 = f32[128,128]{1,0:T(8,128)} custom-call(f32[128,128]{1,0:T(8,128)} %cholesky.665), custom_call_target="Cholesky" | custom-call | tf_op jit(solution)/shard_map/jit(cholesky)/cholesky | solution.py:25
  630.3 11.3 %custom-call.37 = f32[1,128,128]{1,2,0:T(8,128)} custom-call(f32[1,128,128]{2,1,0:T(8,128)} %get-tuple-element.188), custom_call_target="InvertDiagBlocksLowerTriangular" | custom-call | tf_op jit(solution)/shard_map/jit(cholesky)/cholesky | solution.py:25
  645.0 13.2 %cholesky.569 = f32[128,128]{1,0:T(8,128)} custom-call(f32[128,128]{1,0:T(8,128)} %convolution_subtract_fusion.22), custom_call_target="Cholesky" | custom-call | tf_op jit(solution)/shard_map/jit(cholesky)/cholesky | solution.py:25
  671.1 21.1 %custom-call.38 = f32[2,128,128]{1,2,0:T(8,128)} custom-call(f32[2,128,128]{2,1,0:T(8,128)} %get-tuple-element.62), custom_call_target="InvertDiagBlocksLowerTriangular" | custom-call | tf_op jit(solution)/shard_map/jit(_cho_solve)/triangular_solve | solution.py:26
  721.0 13.2 %cholesky.586 = f32[128,128]{1,0:T(8,128)} custom-call(f32[128,128]{1,0:T(8,128)} %cholesky.668), custom_call_target="Cholesky" | custom-call | tf_op jit(solution)/shard_map/jit(cholesky)/cholesky | solution.py:25
  751.9 13.2 %cholesky.603 = f32[128,128]{1,0:T(8,128)} custom-call(f32[128,128]{1,0:T(8,128)} %convolution_subtract_fusion.21), custom_call_target="Cholesky" | custom-call | tf_op jit(solution)/shard_map/jit(cholesky)/cholesky | solution.py:25
  778.6 21.1 %custom-call.40 = f32[2,128,128]{1,2,0:T(8,128)} custom-call(f32[2,128,128]{2,1,0:T(8,128)} %get-tuple-element.63), custom_call_target="InvertDiagBlocksLowerTriangular" | custom-call | tf_op jit(solution)/shard_map/jit(_cho_solve)/triangular_solve | solution.py:26
  833.7 13.2 %cholesky.620 = f32[128,128]{1,0:T(8,128)} custom-call(f32[128,128]{1,0:T(8,128)} %cholesky.671), custom_call_target="Cholesky" | custom-call | tf_op jit(solution)/shard_map/jit(cholesky)/cholesky | solution.py:25
  864.6 13.2 %cholesky.637 = f32[128,128]{1,0:T(8,128)} custom-call(f32[128,128]{1,0:T(8,128)} %convolution_subtract_fusion.20), custom_call_target="Cholesky" | custom-call | tf_op jit(solution)/shard_map/jit(cholesky)/cholesky | solution.py:25
  890.9 21.1 %custom-call.42 = f32[2,128,128]{1,2,0:T(8,128)} custom-call(f32[2,128,128]{2,1,0:T(8,128)} %get-tuple-element.64), custom_call_target="InvertDiagBlocksLowerTriangular" | custom-call | tf_op jit(solution)/shard_map/jit(_cho_solve)/triangular_solve | solution.py:26
  (404 shorter events, 492.8 us)
Async XLA Ops:
  0.0 4.3 copy-start
  4.3 7.0 copy-start.7
  13.2 10.9 %collective-permute-start = (f32[256,384]{0,1:T(8,128)}, f32[256,384]{0,1:T(8,128)}, u32[]{:S(2)}, u32[]{:S(2)}) collective-permute-start(f32[256,384]{0,1:T(8,128)} %convolution_bitcast_fusion), channel_id=1, source_target_pairs={{0,1},{1,0},{2,3},{3,2},{4,5},{5,4},{6,7},{7,6},{8,9},{9,8},{10,11... | collective-permute-start | bytes 1179656 | tf_op jit(solution)/shard_map/ppermute | solution.py:14
  126.7 11.0 %collective-permute-start.1 = (f32[256,384]{0,1:T(8,128)}, f32[256,384]{0,1:T(8,128)}, u32[]{:S(2)}, u32[]{:S(2)}) collective-permute-start(f32[256,384]{0,1:T(8,128)} %convolution_bitcast_fusion.7), channel_id=1, source_target_pairs={{0,2},{2,0},{1,3},{3,1},{4,6},{6,4},{5,7},{7,5},{8,10},{10,8},{9,1... | collective-permute-start | bytes 1179656 | tf_op jit(solution)/shard_map/ppermute | solution.py:14
  226.8 6.3 copy-start.55
  231.8 1.6 copy-start.1
  233.4 2.6 copy-start.11
  236.0 11.6 %collective-permute-start.2 = (f32[256,384]{0,1:T(8,128)}, f32[256,384]{0,1:T(8,128)}, u32[]{:S(2)}, u32[]{:S(2)}) collective-permute-start(f32[256,384]{0,1:T(8,128)} %convolution_bitcast_fusion.6), channel_id=1, source_target_pairs={{0,4},{4,0},{1,5},{5,1},{2,6},{6,2},{3,7},{7,3},{8,12},{12,8},{9,1... | collective-permute-start | bytes 1179656 | tf_op jit(solution)/shard_map/ppermute | solution.py:14
  350.8 9.2 collective-permute-start.3
  449.1 6.3 copy-start.56
  455.8 2.6 copy-start.16
  458.4 20.4 %collective-permute-start.4 = (f32[256,384]{0,1:T(8,128)}, f32[256,384]{0,1:T(8,128)}, u32[]{:S(2)}, u32[]{:S(2)}) collective-permute-start(f32[256,384]{0,1:T(8,128)} %convolution_bitcast_fusion.4), channel_id=1, source_target_pairs={{0,16},{16,0},{1,17},{17,1},{2,18},{18,2},{3,19},{19,3},{4,20},{20... | collective-permute-start | bytes 1179656 | tf_op jit(solution)/shard_map/ppermute | solution.py:14
  581.2 22.5 %collective-permute-start.5 = (f32[256,384]{0,1:T(8,128)}, f32[256,384]{0,1:T(8,128)}, u32[]{:S(2)}, u32[]{:S(2)}) collective-permute-start(f32[256,384]{0,1:T(8,128)} %convolution_bitcast_fusion.3), channel_id=1, source_target_pairs={{0,32},{32,0},{1,33},{33,1},{2,34},{34,2},{3,35},{35,3},{4,36},{36... | collective-permute-start | bytes 1179656 | tf_op jit(solution)/shard_map/ppermute | solution.py:14
  692.2 6.3 copy-start.57
  698.9 2.6 copy-start.21
  701.5 9.2 collective-permute-start.6
  813.5 9.8 %collective-permute-start.7 = (f32[256,384]{0,1:T(8,128)}, f32[256,384]{0,1:T(8,128)}, u32[]{:S(2)}, u32[]{:S(2)}) collective-permute-start(f32[256,384]{0,1:T(8,128)} %convolution_bitcast_fusion.1), channel_id=1, source_target_pairs={{0,128},{128,0},{64,192},{192,64},{1,129},{129,1},{65,193},{193,65... | collective-permute-start | bytes 1179656 | tf_op jit(solution)/shard_map/ppermute | solution.py:14
  912.0 6.4 copy-start.54
  912.0 6.7 copy-start.23
  912.0 6.8 copy-start.25
  913.4 5.8 copy-start.6
  913.4 5.8 copy-start.22
  914.7 4.9 copy-start.18
  914.7 4.9 copy-start.20
  918.4 1.7 copy-start.4
  918.4 1.7 copy-start.17
  918.8 1.7 copy-start.13
  918.8 1.7 copy-start.15
  919.2 1.7 copy-start.2
  919.2 1.7 copy-start.12
  919.6 1.7 copy-start.8
  919.7 1.7 copy-start.10
  (34 other events, 27.1 us)
where the time goes:
time: 945 us; the launch traced here: 929 us
  other arithmetic  556 us (59%)
  local copies, waits for them, and re-layouts  158 us (17%)
  matrix products  117 us (12%)
  waiting for transfers between devices  69.7 us (7%)
  starting transfers between devices  14.9 us (2%)
  between operations  11.1 us (1%)
    another operation x55, other arithmetic, node_update(): lower = jnp.linalg.cholesky(factor)  334 us
    another operation x17, other arithmetic, node_update(): jax.scipy.linalg.cho_solve((lower, True), jnp.concatenate([link, target],...  182 us
    ppermute x8, waiting for transfers between devices, from_partner(): return lax.ppermute(block, axis, route)  69.7 us
    another operation x61, local copies, waits for them, and re-layouts, node_update(): jax.scipy.linalg.cho_solve((lower, True), jnp.concatenate([link, target],...  66.7 us
    another operation x48, matrix products, node_update(): jax.scipy.linalg.cho_solve((lower, True), jnp.concatenate([link, target],...  59.8 us
    unnamed x124, local copies, waits for them, and re-layouts  32.1 us
    another operation x16, matrix products, node_update(): lower = jnp.linalg.cholesky(factor)  27.4 us
  transfers between devices with their start and end apart: 8, of which 7 were waited for; matrix products, arithmetic and copies ran while one was open for 2% of the time, Pallas kernels for 0%

commit v1 on v0

v1 whole, which is shorter than its diff:
```python
import functools
import jax
import jax.numpy as jnp
from jax import lax
from jax.experimental import pallas as pl
from jax.experimental.pallas import tpu as pltpu
from jax.sharding import PartitionSpec as P

BF = jnp.bfloat16
F32 = jnp.float32
MESH = pl.DeviceIdType.MESH
HALF = 128
RANK = 256
NRHS = 128
LEAF = 768
LEVELS = 8
WIDE = RANK + NRHS
TERMS = ((0, 0), (0, 1), (1, 0), (0, 2), (2, 0), (1, 1))


def dot(a, b):
    return jnp.dot(a, b, precision=lax.Precision.HIGHEST, preferred_element_type=F32)


def dot_tn(a, b):
    return lax.dot_general(
        a, b, (((0,), (0,)), ((), ())), precision=lax.Precision.HIGHEST, preferred_element_type=F32
    )


def parts_of(x):
    high = x.astype(BF).astype(F32)
    rest = x - high
    mid = rest.astype(BF).astype(F32)
    return (high, mid, rest - mid)


def rank8_product(rows, solved):
    a, b = parts_of(rows), parts_of(solved)
    left = jnp.concatenate([a[i] for i, _ in TERMS], axis=0).astype(BF)
    right = jnp.concatenate([b[j] for _, j in TERMS], axis=0).astype(BF)
    return lax.dot_general(left, right, (((0,), (0,)), ((), ())), preferred_element_type=F32)


def sweep(a_ref):
    size = a_ref.shape[0]
    tile = (8, size)
    lane = lax.broadcasted_iota(jnp.int32, tile, 1)
    sub = lax.broadcasted_iota(jnp.int32, tile, 0)

    def spread(v):
        return jnp.broadcast_to(v, tile)

    now = a_ref[0:8, :]
    for first in range(0, size, 8):
        here = (lane >= first) & (lane < first + 8)
        columns = [spread(now[:, first + j : first + j + 1]) for j in range(8)]
        entry = {(i, j): spread(columns[j][i : i + 1, :]) for j in range(8) for i in range(j, 8)}
        row = [
            jnp.where(here, jnp.where(lane == first + i, -1.0, 0.0), spread(now[i : i + 1, :]))
            for i in range(8)
        ]
        lower, pivot = {}, []
        for k in range(8):
            pivot.append(1.0 / entry[k, k])
            for i in range(k + 1, 8):
                lower[i, k] = entry[i, k] * pivot[k]
            for i in range(k + 1, 8):
                for j in range(k + 1, i + 1):
                    entry[i, j] = entry[i, j] - lower[i, k] * entry[j, k]
                row[i] = row[i] - lower[i, k] * row[k]
        row = [r * p for r, p in zip(row, pivot)]
        for k in range(7, -1, -1):
            for i in range(k):
                row[i] = row[i] - lower[k, i] * row[k]
        solved = row[7]
        for i in range(7):
            solved = jnp.where(sub == i, row[i], solved)
        change = rank8_product(now, solved)
        after = None
        if first + 8 < size:
            after = a_ref[first + 8 : first + 16, :]
            terms = [spread(after[:, first + i : first + i + 1]) * row[i] for i in range(8)]
            while len(terms) > 1:
                terms = [terms[q] + terms[q + 1] for q in range(0, len(terms), 2)]
            after = jnp.where(here, 0.0, after) - terms[0]
        for q in range(0, size, 8):
            if q == first:
                a_ref[q : q + 8, :] = solved
            elif q == first + 8:
                a_ref[q : q + 8, :] = after
            else:
                old = jnp.where(here, 0.0, a_ref[q : q + 8, :])
                a_ref[q : q + 8, :] = old - change[q : q + 8, :]
        now = after


PIECES = (
    (slice(0, 128), slice(0, 128)),
    (slice(0, 128), slice(128, 256)),
    (slice(128, 256), slice(128, 256)),
    (slice(0, 256), slice(256, 384)),
)


def partner_of(level):
    dev, grp = lax.axis_index("dev"), lax.axis_index("grp")
    core, x, z = dev % 2, (dev // 2) % 4, dev // 8
    one = lambda flag, yes, no: jnp.where(flag, yes, no)
    new_core = one(level == 1, 1 - core, core)
    flip_x = x + 1 - 2 * (x % 2)
    new_x = one(level == 2, flip_x, one(level == 3, 3 - x, x))
    flip_z0 = z + 1 - 2 * (z % 2)
    flip_z1 = z + 2 - 4 * ((z // 2) % 2)
    new_z = one(level == 4, flip_z0, one(level == 5, flip_z1, one(level == 6, 7 - z, z)))
    flip_y = grp + 1 - 2 * (grp % 2)
    new_y = one(level == 7, flip_y, one(level == 8, 3 - grp, grp))
    return (new_y, (new_z * 4 + new_x) * 2 + new_core)


def kernel(
    inverse_hbm, basis_hbm, block_hbm, link_hbm, loads_hbm, order_ref, out_hbm,
    inverse, basis, block, link, loads, hot, leaf_w, leaf_y, lift, received, gain, part, value, low, high, result,
    in_sem, send_sem, recv_sem, out_sem,
):
    loaded = []
    for i, (src, dst) in enumerate(
        [(basis_hbm, basis), (inverse_hbm, inverse), (loads_hbm, loads), (block_hbm, block), (link_hbm, link)]
    ):
        loaded.append(pltpu.make_async_copy(src, dst, in_sem.at[i]))
        loaded[-1].start()
    barrier = pltpu.get_barrier_semaphore()
    for level in range(1, LEVELS + 1):
        pl.semaphore_signal(barrier, inc=1, device_id=partner_of(level), device_id_type=MESH)

    def exchange(level, piece):
        rows, columns = PIECES[piece]
        return pltpu.make_async_remote_copy(
            src_ref=lift.at[rows, columns],
            dst_ref=received.at[level - 1, rows, columns],
            send_sem=send_sem.at[level - 1, piece],
            recv_sem=recv_sem.at[level - 1, piece],
            device_id=partner_of(level),
            device_id_type=MESH,
        )

    loaded[0].wait()
    loaded[1].wait()
    leaf_w[...] = dot(inverse[...], basis[...])
    upper = dot_tn(basis[...], leaf_w[...])
    lift[:, :RANK] = upper
    pl.semaphore_wait(barrier, LEVELS)
    for piece in range(3):
        exchange(1, piece).start()
    loaded[2].wait()
    rows = lax.broadcasted_iota(jnp.int32, (LEAF, LEAF), 0)
    hot[...] = jnp.where(rows == order_ref[...], 1.0, 0.0).astype(BF)
    pieces = parts_of(loads[...])
    stacked = jnp.concatenate([p.astype(BF) for p in pieces], axis=1)
    picked = lax.dot_general(hot[...], stacked, (((0,), (0,)), ((), ())), preferred_element_type=F32)
    reordered = (picked[:, :NRHS] + picked[:, NRHS : 2 * NRHS]) + picked[:, 2 * NRHS :]
    leaf_y[...] = dot(inverse[...], reordered)
    lift[:, RANK:] = dot_tn(basis[...], leaf_y[...])
    exchange(1, 3).start()
    loaded[3].wait()
    loaded[4].wait()

    def node(level, carry):
        slot = level - 1
        base = slot * RANK
        top = pl.ds(pl.multiple_of(base, RANK), HALF)
        bottom = pl.ds(pl.multiple_of(base + HALF, HALF), HALF)

        def joined(rows, columns):
            return lift[rows, columns] + received[slot, rows, columns]

        exchange(level, 0).wait_recv()
        low[...] = block[top, 0:HALF] + joined(*PIECES[0])
        sweep(low)
        for piece in range(1, 4):
            exchange(level, piece).wait_recv()
        sign = 2.0 * (level % 2).astype(F32) - 1.0
        target = sign * joined(*PIECES[3])
        cross = block[top, HALF:RANK] + joined(*PIECES[1])
        first = -low[...]
        through = dot(first, cross)
        high[...] = block[bottom, HALF:RANK] + joined(*PIECES[2]) - dot_tn(cross, through)
        link_low, link_high = link[top, :], link[bottom, :]
        given_low = jnp.concatenate([link_low, target[:HALF]], axis=1)
        given_high = jnp.concatenate([link_high, target[HALF:]], axis=1)
        solved_low = dot(first, given_low)
        rest = given_high - dot_tn(cross, solved_low)
        lifted = dot_tn(link_low, solved_low)
        sweep(high)
        solved_high = dot(-high[...], rest)
        lifted = lifted + dot_tn(rest[:, :RANK], solved_high)
        for piece in range(4):
            exchange(level, piece).wait_send()
        lift[...] = lifted

        @pl.when(level < LEVELS)
        def _():
            for piece in range(4):
                exchange(level + 1, piece).start()

        solved_low = solved_low - dot(through, solved_high)
        gain[slot, 0:HALF, :] = solved_low[:, :RANK]
        gain[slot, HALF:RANK, :] = solved_high[:, :RANK]
        part[slot, 0:HALF, :] = solved_low[:, RANK:]
        part[slot, HALF:RANK, :] = solved_high[:, RANK:]
        return carry

    lax.fori_loop(1, LEVELS + 1, node, 0)

    value[...] = part[LEVELS - 1]

    def down(step, carry):
        level = LEVELS - 1 - step
        sign = 1.0 - 2.0 * (level % 2).astype(F32)
        value[...] = part[level - 1] - sign * dot(gain[level - 1], value[...])
        return carry

    lax.fori_loop(0, LEVELS - 1, down, 0)
    local = leaf_y[...] - dot(leaf_w[...], value[...])
    stacked = jnp.concatenate([p.astype(BF) for p in parts_of(local)], axis=1)
    placed = jnp.dot(hot[...], stacked, preferred_element_type=F32)
    result[...] = (placed[:, :NRHS] + placed[:, NRHS : 2 * NRHS]) + placed[:, 2 * NRHS :]
    done = pltpu.make_async_copy(result, out_hbm, out_sem)
    done.start()
    done.wait()


def shards(leaf_inverse, leaf_basis, node_block, node_link, loads, order):
    hbm = pl.BlockSpec(memory_space=pl.ANY)
    return pl.pallas_call(
        kernel,
        out_shape=jax.ShapeDtypeStruct(loads.shape, F32),
        in_specs=[hbm] * 5 + [pl.BlockSpec(memory_space=pltpu.VMEM)],
        out_specs=hbm,
        scratch_shapes=[
            pltpu.VMEM((LEAF, LEAF), F32),
            pltpu.VMEM((LEAF, RANK), F32),
            pltpu.VMEM((LEVELS * RANK, RANK), F32),
            pltpu.VMEM((LEVELS * RANK, RANK), F32),
            pltpu.VMEM((LEAF, NRHS), F32),
            pltpu.VMEM((LEAF, LEAF), BF),
            pltpu.VMEM((LEAF, RANK), F32),
            pltpu.VMEM((LEAF, NRHS), F32),
            pltpu.VMEM((RANK, WIDE), F32),
            pltpu.VMEM((LEVELS, RANK, WIDE), F32),
            pltpu.VMEM((LEVELS, RANK, RANK), F32),
            pltpu.VMEM((LEVELS, RANK, NRHS), F32),
            pltpu.VMEM((RANK, NRHS), F32),
            pltpu.VMEM((HALF, HALF), F32),
            pltpu.VMEM((HALF, HALF), F32),
            pltpu.VMEM((LEAF, NRHS), F32),
            pltpu.SemaphoreType.DMA((5,)),
            pltpu.SemaphoreType.DMA((LEVELS, 4)),
            pltpu.SemaphoreType.DMA((LEVELS, 4)),
            pltpu.SemaphoreType.DMA,
        ],
        compiler_params=pltpu.CompilerParams(
            collective_id=0, has_side_effects=True, vmem_limit_bytes=48 * 1024 * 1024
        ),
        cost_estimate=pl.CostEstimate(flops=4_000_000_000, bytes_accessed=8_000_000, transcendentals=0),
    )(leaf_inverse, leaf_basis, node_block, node_link, loads, order)


def solution(mesh):
    spec = P(("grp", "dev"), None)
    return jax.shard_map(shards, mesh=mesh, in_specs=(spec,) * 6, out_specs=spec, check_vma=False)
```

time: 945 us -> 146 us (0.15); the launches traced: 929 us -> 145 us
  other arithmetic: 556 us -> 0 us
  local copies, waits for them, and re-layouts: 158 us -> 6.74 us
  Pallas kernels: 0 us -> 138 us
  matrix products: 117 us -> 0 us
  waiting for transfers between devices: 69.7 us -> 0 us
  starting transfers between devices: 14.9 us -> 0 us
  between operations: 11.1 us -> 0.01 us
    another operation x72 -> x0, other arithmetic: 517 us -> none  [the longest x55 334 us: node_update(): lower = jnp.linalg.cholesky(factor)]
    pallas_call x0 -> x1, Pallas kernels: none -> 138 us  [shards(): pl.pallas_call(kernel, out_shape=jax.ShapeDtypeStruct(loads.shape, F32),...]
    another operation x64 -> x0, matrix products: 87.3 us -> none  [the longest x48 59.8 us: node_update(): jax.scipy.linalg.cho_solve((lower, True), jnp.concatenate([link, target],...]
    another operation x77 -> x0, local copies, waits for them, and re-layouts: 84.2 us -> none  [the longest x61 66.7 us: node_update(): jax.scipy.linalg.cho_solve((lower, True), jnp.concatenate([link, target],...]
    ppermute x8 -> x0, waiting for transfers between devices: 69.7 us -> none  [from_partner(): return lax.ppermute(block, axis, route)]
    dot_general x17 -> x0, matrix products: 29.7 us -> none  [the longest x7 16.9 us: node_update(): lifted_rows = jnp.dot(link.T, solved, precision=lax.Precision.HIGHEST)]
    unnamed x124 -> x11, local copies, waits for them, and re-layouts: 32.1 us -> 6.74 us
    add x12 -> x0, local copies, waits for them, and re-layouts: 20.9 us -> none  [the longest x8 14.3 us: node_update(): factor = block + from_left[:, :width] + from_right[:, :width]]
  transfers between devices with their start and end apart: 8 -> 0, of which waited for: 7 -> 0; matrix products, arithmetic and copies ran while one was open for 2% -> 0% of each run, Pallas kernels for 0% -> 0%
where the time goes in v1:
time: 146 us; the launch traced here: 145 us
  Pallas kernels  138 us (95%)
  local copies, waits for them, and re-layouts  6.74 us (5%)
    pallas_call x1, Pallas kernels, shards(): pl.pallas_call(kernel, out_shape=jax.ShapeDtypeStruct(loads.shape, F32),...  138 us
    unnamed x11, local copies, waits for them, and re-layouts  6.74 us

profile of v1, /device:TPU:1, one launch (start us, length us, event | category | flops | bytes accessed | tf_op | source)
XLA Modules:
  0.0 145.2 jit_solution(14371442713038527069)
XLA Ops:
  0.0 0.0 copy-start
  0.0 1.6 %copy-done = f32[2048,256]{1,0:T(8,128)S(1)} copy-done((f32[2048,256]{1,0:T(8,128)S(1)}, f32[2048,256]{1,0:T(8,128)}, u32[]{:S(2)}) %copy-start) | copy-done | bytes 2097176
  1.6 0.0 copy-start.1
  1.6 1.6 %copy-done.1 = f32[2048,256]{1,0:T(8,128)S(1)} copy-done((f32[2048,256]{1,0:T(8,128)S(1)}, f32[2048,256]{1,0:T(8,128)}, u32[]{:S(2)}) %copy-start.1) | copy-done | bytes 2097176
  3.2 0.0 copy-start.2
  3.2 1.1 copy-done.2
  4.3 0.0 copy-start.3
  4.3 1.0 copy-done.3
  5.3 0.0 copy-start.4
  5.3 0.7 copy-done.4
  6.0 138.4 %shard_map.64 = f32[768,128]{1,0:T(8,128)S(1)} custom-call(f32[768,768]{1,0:T(8,128)} %inverse_hbm.1, f32[768,256]{1,0:T(8,128)S(1)} %copy-done.2, f32[2048,256]{1,0:T(8,128)S(1)} %copy-done, f32[2048,256]{1,0:T(8,128)S(1)} %copy-done.1, f32[768,128]{1,0:T(8,128)S(1)} %copy-done.3, s32[1,768]{1,0:T(1,128)S(1)} %copy-done.4), custom_call_target="tpu_custom_call" | custom-call | flops 4000000000 | bytes 8000000 | tf_op jit(solution)/shard_map/pallas_call | solution.py:235
  144.4 0.7 copy.8
Async XLA Ops:
  0.0 1.6 %copy-start = (f32[2048,256]{1,0:T(8,128)S(1)}, f32[2048,256]{1,0:T(8,128)}, u32[]{:S(2)}) copy-start(f32[2048,256]{1,0:T(8,128)} %block_hbm.1) | copy-start | bytes 6291460
  1.6 1.6 %copy-start.1 = (f32[2048,256]{1,0:T(8,128)S(1)}, f32[2048,256]{1,0:T(8,128)}, u32[]{:S(2)}) copy-start(f32[2048,256]{1,0:T(8,128)} %link_hbm.1) | copy-start | bytes 6291460
  3.2 1.1 copy-start.2
  4.3 1.0 copy-start.3
  5.3 0.7 copy-start.4

commit v2 on v1

--- a/solution.py
+++ b/solution.py
@@ -18,14 +18,32 @@
 TERMS = ((0, 0), (0, 1), (1, 0), (0, 2), (2, 0), (1, 1))
 
 
+def halves(x):
+    high = x.astype(BF)
+    return high, (x - high.astype(F32)).astype(BF)
+
+
 def dot(a, b):
-    return jnp.dot(a, b, precision=lax.Precision.HIGHEST, preferred_element_type=F32)
+    ah, al = halves(a)
+    bh, bl = halves(b)
+    one = lambda p, q: jnp.dot(p, q, preferred_element_type=F32)
+    return one(ah, bh) + (one(ah, bl) + one(al, bh))
 
 
 def dot_tn(a, b):
-    return lax.dot_general(
-        a, b, (((0,), (0,)), ((), ())), precision=lax.Precision.HIGHEST, preferred_element_type=F32
-    )
+    ah, al = halves(a)
+    bh, bl = halves(b)
+    one = lambda p, q: lax.dot_general(p, q, (((0,), (0,)), ((), ())), preferred_element_type=F32)
+    return one(ah, bh) + (one(ah, bl) + one(al, bh))
+
+
+def dot_tn_exact(a, b):
+    return lax.dot_general(a, b, (((0,), (0,)), ((), ())), preferred_element_type=F32)
+
+
+def whole(x):
+    size = x.shape[1] // 3
+    return (x[:, :size] + x[:, size : 2 * size]) + x[:, 2 * size :]
 
 
 def parts_of(x):
@@ -51,10 +69,13 @@
     def spread(v):
         return jnp.broadcast_to(v, tile)
 
+    def column(v, j):
+        return jnp.take_along_axis(v, jnp.full(tile, j, jnp.int32), axis=1)
+
     now = a_ref[0:8, :]
     for first in range(0, size, 8):
         here = (lane >= first) & (lane < first + 8)
-        columns = [spread(now[:, first + j : first + j + 1]) for j in range(8)]
+        columns = [column(now, first + j) for j in range(8)]
         entry = {(i, j): spread(columns[j][i : i + 1, :]) for j in range(8) for i in range(j, 8)}
         row = [
             jnp.where(here, jnp.where(lane == first + i, -1.0, 0.0), spread(now[i : i + 1, :]))
@@ -80,7 +101,7 @@
         after = None
         if first + 8 < size:
             after = a_ref[first + 8 : first + 16, :]
-            terms = [spread(after[:, first + i : first + i + 1]) * row[i] for i in range(8)]
+            terms = [column(after, first + i) * row[i] for i in range(8)]
             while len(terms) > 1:
                 terms = [terms[q] + terms[q + 1] for q in range(0, len(terms), 2)]
             after = jnp.where(here, 0.0, after) - terms[0]
@@ -147,23 +168,29 @@
     loaded[0].wait()
     loaded[1].wait()
     leaf_w[...] = dot(inverse[...], basis[...])
-    upper = dot_tn(basis[...], leaf_w[...])
-    lift[:, :RANK] = upper
-    pl.semaphore_wait(barrier, LEVELS)
     for piece in range(3):
+        rows, columns = PIECES[piece]
+        lift[rows, columns] = dot_tn(basis[:, rows], leaf_w[:, columns])
+        if piece == 0:
+            pl.semaphore_wait(barrier, LEVELS)
         exchange(1, piece).start()
-    loaded[2].wait()
-    rows = lax.broadcasted_iota(jnp.int32, (LEAF, LEAF), 0)
-    hot[...] = jnp.where(rows == order_ref[...], 1.0, 0.0).astype(BF)
-    pieces = parts_of(loads[...])
-    stacked = jnp.concatenate([p.astype(BF) for p in pieces], axis=1)
-    picked = lax.dot_general(hot[...], stacked, (((0,), (0,)), ((), ())), preferred_element_type=F32)
-    reordered = (picked[:, :NRHS] + picked[:, NRHS : 2 * NRHS]) + picked[:, 2 * NRHS :]
-    leaf_y[...] = dot(inverse[...], reordered)
-    lift[:, RANK:] = dot_tn(basis[...], leaf_y[...])
-    exchange(1, 3).start()
-    loaded[3].wait()
-    loaded[4].wait()
+    for copy in loaded[2:]:
+        copy.wait()
+
+    def leaf_loads():
+        rows = lax.broadcasted_iota(jnp.int32, (LEAF, LEAF), 0)
+        hot[...] = jnp.where(rows == order_ref[...], 1.0, 0.0).astype(BF)
+        stacked = jnp.concatenate([p.astype(BF) for p in parts_of(loads[...])], axis=1)
+        picked = dot_tn_exact(hot[...], stacked)
+        leaf_y[...] = dot(inverse[...], whole(picked))
+        lift[:, RANK:] = dot_tn(basis[...], leaf_y[...])
+        exchange(1, 3).start()
+
+    def to_initial_order():
+        stacked = jnp.concatenate([p.astype(BF) for p in parts_of(leaf_y[...])], axis=1)
+        leaf_y[...] = whole(jnp.dot(hot[...], stacked, preferred_element_type=F32))
+        stacked = jnp.concatenate([p.astype(BF) for p in parts_of(leaf_w[...])], axis=1)
+        leaf_w[...] = whole(jnp.dot(hot[...], stacked, preferred_element_type=F32))
 
     def node(level, carry):
         slot = level - 1
@@ -177,37 +204,50 @@
         exchange(level, 0).wait_recv()
         low[...] = block[top, 0:HALF] + joined(*PIECES[0])
         sweep(low)
-        for piece in range(1, 4):
-            exchange(level, piece).wait_recv()
+        exchange(level, 1).wait_recv()
+        exchange(level, 2).wait_recv()
+        first = -low[...]
+        cross = block[top, HALF:RANK] + joined(*PIECES[1])
+        through = dot(first, cross)
+        high[...] = block[bottom, HALF:RANK] + joined(*PIECES[2]) - dot_tn(cross, through)
+        link_low = link[top, :]
+        solved_low = dot(first, link_low)
+        rest = link[bottom, :] - dot_tn(cross, solved_low)
+        lifted = [
+            dot_tn(link_low[:, rows], solved_low[:, columns]) for rows, columns in PIECES[:3]
+        ]
+        sweep(high)
+        second = -high[...]
+        solved_high = dot(second, rest)
+        for piece in range(3):
+            rows, columns = PIECES[piece]
+            lifted[piece] += dot_tn(rest[:, rows], solved_high[:, columns])
+            exchange(level, piece).wait_send()
+            lift[rows, columns] = lifted[piece]
+
+            @pl.when(level < LEVELS)
+            def _():
+                exchange(level + 1, piece).start()
+
+        gain[slot, 0:HALF, :] = solved_low - dot(through, solved_high)
+        gain[slot, HALF:RANK, :] = solved_high
+        pl.when(level == 1)(leaf_loads)
+        pl.when(level == 2)(to_initial_order)
+        exchange(level, 3).wait_recv()
         sign = 2.0 * (level % 2).astype(F32) - 1.0
         target = sign * joined(*PIECES[3])
-        cross = block[top, HALF:RANK] + joined(*PIECES[1])
-        first = -low[...]
-        through = dot(first, cross)
-        high[...] = block[bottom, HALF:RANK] + joined(*PIECES[2]) - dot_tn(cross, through)
-        link_low, link_high = link[top, :], link[bottom, :]
-        given_low = jnp.concatenate([link_low, target[:HALF]], axis=1)
-        given_high = jnp.concatenate([link_high, target[HALF:]], axis=1)
-        solved_low = dot(first, given_low)
-        rest = given_high - dot_tn(cross, solved_low)
-        lifted = dot_tn(link_low, solved_low)
-        sweep(high)
-        solved_high = dot(-high[...], rest)
-        lifted = lifted + dot_tn(rest[:, :RANK], solved_high)
-        for piece in range(4):
-            exchange(level, piece).wait_send()
-        lift[...] = lifted
+        part_low = dot(first, target[:HALF])
+        part_rest = target[HALF:] - dot_tn(cross, part_low)
+        part_high = dot(second, part_rest)
+        exchange(level, 3).wait_send()
+        lift[:, RANK:] = dot_tn(link_low, part_low) + dot_tn(rest, part_high)
 
         @pl.when(level < LEVELS)
         def _():
-            for piece in range(4):
-                exchange(level + 1, piece).start()
-
-        solved_low = solved_low - dot(through, solved_high)
-        gain[slot, 0:HALF, :] = solved_low[:, :RANK]
-        gain[slot, HALF:RANK, :] = solved_high[:, :RANK]
-        part[slot, 0:HALF, :] = solved_low[:, RANK:]
-        part[slot, HALF:RANK, :] = solved_high[:, RANK:]
+            exchange(level + 1, 3).start()
+
+        part[slot, 0:HALF, :] = part_low - dot(through, part_high)
+        part[slot, HALF:RANK, :] = part_high
         return carry
 
     lax.fori_loop(1, LEVELS + 1, node, 0)
@@ -221,17 +261,14 @@
         return carry
 
     lax.fori_loop(0, LEVELS - 1, down, 0)
-    local = leaf_y[...] - dot(leaf_w[...], value[...])
-    stacked = jnp.concatenate([p.astype(BF) for p in parts_of(local)], axis=1)
-    placed = jnp.dot(hot[...], stacked, preferred_element_type=F32)
-    result[...] = (placed[:, :NRHS] + placed[:, NRHS : 2 * NRHS]) + placed[:, 2 * NRHS :]
+    result[...] = leaf_y[...] - dot(leaf_w[...], value[...])
     done = pltpu.make_async_copy(result, out_hbm, out_sem)
     done.start()
     done.wait()
 
 
 def shards(leaf_inverse, leaf_basis, node_block, node_link, loads, order):
-    hbm = pl.BlockSpec(memory_space=pl.ANY)
+    hbm = pl.BlockSpec(memory_space=pltpu.HBM)
     return pl.pallas_call(
         kernel,
         out_shape=jax.ShapeDtypeStruct(loads.shape, F32),
@@ -260,7 +297,7 @@
             pltpu.SemaphoreType.DMA,
         ],
         compiler_params=pltpu.CompilerParams(
-            collective_id=0, has_side_effects=True, vmem_limit_bytes=48 * 1024 * 1024
+            collective_id=0, has_side_effects=True, vmem_limit_bytes=63 * 1024 * 1024
         ),
         cost_estimate=pl.CostEstimate(flops=4_000_000_000, bytes_accessed=8_000_000, transcendentals=0),
     )(leaf_inverse, leaf_basis, node_block, node_link, loads, order)

time: 146 us -> 117 us (0.80)
  Pallas kernels: 138 us -> 113 us
  local copies, waits for them, and re-layouts: 6.74 us -> 1.77 us
    pallas_call x1, Pallas kernels: 138 us -> 113 us  [shards(): pl.pallas_call(kernel, out_shape=jax.ShapeDtypeStruct(loads.shape, F32),...]
    unnamed x11 -> x1, local copies, waits for them, and re-layouts: 6.74 us -> 1.77 us
where the time goes in v2:
time: 117 us; the launch traced here: 115 us
  Pallas kernels  113 us (97%)
  local copies, waits for them, and re-layouts  1.77 us (2%)
    pallas_call x1, Pallas kernels, shards(): pl.pallas_call(kernel, out_shape=jax.ShapeDtypeStruct(loads.shape, F32),...  113 us

profile of v2, /device:TPU:1, one launch (start us, length us, event | category | flops | bytes accessed | tf_op | source)
XLA Modules:
  0.0 115.0 jit_solution(17685696426494551072)
XLA Ops:
  0.0 113.2 %shard_map.64 = f32[768,128]{1,0:T(8,128)} custom-call(f32[768,768]{1,0:T(8,128)} %inverse_hbm.1, f32[768,256]{1,0:T(8,128)} %basis_hbm.1, f32[2048,256]{1,0:T(8,128)} %block_hbm.1, f32[2048,256]{1,0:T(8,128)} %link_hbm.1, f32[768,128]{1,0:T(8,128)} %loads_hbm.1, s32[1,768]{1,0:T(1,128)} %order_ref.1), custom_call_target="tpu_custom_call" | custom-call | flops 4000000000 | bytes 8000000 | tf_op jit(solution)/shard_map/pallas_call | solution.py:272
  113.2 1.8 %copy.8 = f32[768,128]{1,0:T(8,128)} copy(f32[768,128]{1,0:T(8,128)} %shard_map.64) | data formatting | bytes 786432

commit v3 on v2

--- a/solution.py
+++ b/solution.py
@@ -14,6 +14,7 @@
 NRHS = 128
 LEAF = 768
 LEVELS = 8
+AHEAD = 3
 WIDE = RANK + NRHS
 TERMS = ((0, 0), (0, 1), (1, 0), (0, 2), (2, 0), (1, 1))
 
@@ -62,34 +63,47 @@
 
 def sweep(a_ref):
     size = a_ref.shape[0]
+    groups = size // 8
     tile = (8, size)
     lane = lax.broadcasted_iota(jnp.int32, tile, 1)
     sub = lax.broadcasted_iota(jnp.int32, tile, 0)
 
-    def spread(v):
-        return jnp.broadcast_to(v, tile)
+    def spread(v, i):
+        return jnp.broadcast_to(v[i : i + 1, :], tile)
 
     def column(v, j):
         return jnp.take_along_axis(v, jnp.full(tile, j, jnp.int32), axis=1)
 
-    now = a_ref[0:8, :]
-    for first in range(0, size, 8):
+    near = {g: a_ref[8 * g : 8 * g + 8, :] for g in range(AHEAD + 1)}
+    diag = [column(near[0], j) for j in range(8)]
+    cross = [column(near[1], j) for j in range(8)]
+    for step in range(groups):
+        first = 8 * step
+        now = near.pop(step)
         here = (lane >= first) & (lane < first + 8)
-        columns = [column(now, first + j) for j in range(8)]
-        entry = {(i, j): spread(columns[j][i : i + 1, :]) for j in range(8) for i in range(j, 8)}
+        more = step + 1 < groups
+        entry = {(i, j): spread(diag[j], i) for j in range(8) for i in range(j, 8)}
         row = [
-            jnp.where(here, jnp.where(lane == first + i, -1.0, 0.0), spread(now[i : i + 1, :]))
+            jnp.where(here, jnp.where(lane == first + i, -1.0, 0.0), spread(now, i))
             for i in range(8)
         ]
+        if more:
+            diag = [column(near[step + 1], first + 8 + j) for j in range(8)]
+            reduced = list(cross)
         lower, pivot = {}, []
         for k in range(8):
             pivot.append(1.0 / entry[k, k])
             for i in range(k + 1, 8):
                 lower[i, k] = entry[i, k] * pivot[k]
-            for i in range(k + 1, 8):
                 for j in range(k + 1, i + 1):
                     entry[i, j] = entry[i, j] - lower[i, k] * entry[j, k]
+                if more:
+                    reduced[i] = reduced[i] - lower[i, k] * reduced[k]
+            for i in range(k + 1, 8):
                 row[i] = row[i] - lower[i, k] * row[k]
+            if more:
+                scaled = reduced[k] * pivot[k]
+                diag = [diag[j] - scaled * spread(reduced[k], j) for j in range(8)]
         row = [r * p for r, p in zip(row, pivot)]
         for k in range(7, -1, -1):
             for i in range(k):
@@ -98,22 +112,23 @@
         for i in range(7):
             solved = jnp.where(sub == i, row[i], solved)
         change = rank8_product(now, solved)
-        after = None
-        if first + 8 < size:
-            after = a_ref[first + 8 : first + 16, :]
-            terms = [column(after, first + i) * row[i] for i in range(8)]
+        later = {}
+        for g in range(step + 1, min(groups, step + AHEAD + 1)):
+            old = near[g] if g in near else a_ref[8 * g : 8 * g + 8, :]
+            columns = cross if g == step + 1 else [column(old, first + i) for i in range(8)]
+            terms = [c * r for c, r in zip(columns, row)]
             while len(terms) > 1:
                 terms = [terms[q] + terms[q + 1] for q in range(0, len(terms), 2)]
-            after = jnp.where(here, 0.0, after) - terms[0]
-        for q in range(0, size, 8):
-            if q == first:
-                a_ref[q : q + 8, :] = solved
-            elif q == first + 8:
-                a_ref[q : q + 8, :] = after
-            else:
-                old = jnp.where(here, 0.0, a_ref[q : q + 8, :])
-                a_ref[q : q + 8, :] = old - change[q : q + 8, :]
-        now = after
+            later[g] = jnp.where(here, 0.0, old) - terms[0]
+        for g in range(groups):
+            rows = slice(8 * g, 8 * g + 8)
+            if g == step:
+                a_ref[rows, :] = solved
+            elif g not in later:
+                a_ref[rows, :] = jnp.where(here, 0.0, a_ref[rows, :]) - change[rows, :]
+        near = later
+        if step + 2 < groups:
+            cross = [column(near[step + 2], first + 8 + i) for i in range(8)]
 
 
 PIECES = (
@@ -165,6 +180,30 @@
             device_id_type=MESH,
         )
 
+    core = lax.axis_index("dev") % 2
+    mine = pl.ds(pl.multiple_of(core * HALF, HALF), HALF)
+    sides = slice(RANK, WIDE)
+
+    def exchange_half(level):
+        return pltpu.make_async_remote_copy(
+            src_ref=lift.at[mine, sides],
+            dst_ref=received.at[level - 1, mine, sides],
+            send_sem=send_sem.at[level - 1, 3],
+            recv_sem=recv_sem.at[level - 1, 3],
+            device_id=partner_of(level),
+            device_id_type=MESH,
+        )
+
+    def relay_half(level):
+        return pltpu.make_async_remote_copy(
+            src_ref=received.at[level - 1, mine, sides],
+            dst_ref=received.at[level - 1, mine, sides],
+            send_sem=send_sem.at[level - 1, 4],
+            recv_sem=recv_sem.at[level - 1, 4],
+            device_id=partner_of(1),
+            device_id_type=MESH,
+        )
+
     loaded[0].wait()
     loaded[1].wait()
     leaf_w[...] = dot(inverse[...], basis[...])
@@ -176,13 +215,13 @@
         exchange(1, piece).start()
     for copy in loaded[2:]:
         copy.wait()
+    rows = lax.broadcasted_iota(jnp.int32, (LEAF, LEAF), 0)
+    hot[...] = jnp.where(rows == order_ref[...], 1.0, 0.0).astype(BF)
+    stacked = jnp.concatenate([p.astype(BF) for p in parts_of(loads[...])], axis=1)
+    leaf_y[...] = whole(dot_tn_exact(hot[...], stacked))
 
     def leaf_loads():
-        rows = lax.broadcasted_iota(jnp.int32, (LEAF, LEAF), 0)
-        hot[...] = jnp.where(rows == order_ref[...], 1.0, 0.0).astype(BF)
-        stacked = jnp.concatenate([p.astype(BF) for p in parts_of(loads[...])], axis=1)
-        picked = dot_tn_exact(hot[...], stacked)
-        leaf_y[...] = dot(inverse[...], whole(picked))
+        leaf_y[...] = dot(inverse[...], leaf_y[...])
         lift[:, RANK:] = dot_tn(basis[...], leaf_y[...])
         exchange(1, 3).start()
 
@@ -218,33 +257,50 @@
         ]
         sweep(high)
         second = -high[...]
-        solved_high = dot(second, rest)
         for piece in range(3):
-            rows, columns = PIECES[piece]
-            lifted[piece] += dot_tn(rest[:, rows], solved_high[:, columns])
             exchange(level, piece).wait_send()
-            lift[rows, columns] = lifted[piece]
-
-            @pl.when(level < LEVELS)
-            def _():
+
+        @pl.when(level < LEVELS)
+        def _():
+            solved_high = dot(second, rest)
+            for piece in range(3):
+                rows, columns = PIECES[piece]
+                lift[rows, columns] = lifted[piece] + dot_tn(rest[:, rows], solved_high[:, columns])
                 exchange(level + 1, piece).start()
-
-        gain[slot, 0:HALF, :] = solved_low - dot(through, solved_high)
-        gain[slot, HALF:RANK, :] = solved_high
+            gain[slot, HALF:RANK, :] = solved_high
+
         pl.when(level == 1)(leaf_loads)
-        pl.when(level == 2)(to_initial_order)
-        exchange(level, 3).wait_recv()
+
+        @pl.when(level > 1)
+        def _():
+            exchange_half(level).wait_recv()
+            relay_half(level).start()
+
+        pl.when(level == 5)(to_initial_order)
+
+        @pl.when(level < LEVELS)
+        def _():
+            gain[slot, 0:HALF, :] = solved_low - dot(through, gain[slot, HALF:RANK, :])
+
+        @pl.when(level == 1)
+        def _():
+            exchange(1, 3).wait()
+
+        @pl.when(level > 1)
+        def _():
+            relay_half(level).wait()
+            exchange_half(level).wait_send()
+
         sign = 2.0 * (level % 2).astype(F32) - 1.0
         target = sign * joined(*PIECES[3])
         part_low = dot(first, target[:HALF])
         part_rest = target[HALF:] - dot_tn(cross, part_low)
         part_high = dot(second, part_rest)
-        exchange(level, 3).wait_send()
-        lift[:, RANK:] = dot_tn(link_low, part_low) + dot_tn(rest, part_high)
 
         @pl.when(level < LEVELS)
         def _():
-            exchange(level + 1, 3).start()
+            lift[:, RANK:] = dot_tn(link_low, part_low) + dot_tn(rest, part_high)
+            exchange_half(level + 1).start()
 
         part[slot, 0:HALF, :] = part_low - dot(through, part_high)
         part[slot, HALF:RANK, :] = part_high
@@ -292,8 +348,8 @@
             pltpu.VMEM((HALF, HALF), F32),
             pltpu.VMEM((LEAF, NRHS), F32),
             pltpu.SemaphoreType.DMA((5,)),
-            pltpu.SemaphoreType.DMA((LEVELS, 4)),
-            pltpu.SemaphoreType.DMA((LEVELS, 4)),
+            pltpu.SemaphoreType.DMA((LEVELS, 5)),
+            pltpu.SemaphoreType.DMA((LEVELS, 5)),
             pltpu.SemaphoreType.DMA,
         ],
         compiler_params=pltpu.CompilerParams(

time: 117 us -> 105 us (0.90); the launches traced: 115 us -> 105 us
  Pallas kernels: 113 us -> 103 us
    pallas_call x1, Pallas kernels: 113 us -> 103 us  [shards(): pl.pallas_call(kernel, out_shape=jax.ShapeDtypeStruct(loads.shape, F32),...]
where the time goes in v3:
time: 105 us
  Pallas kernels  103 us (98%)
  local copies, waits for them, and re-layouts  1.77 us (2%)
    pallas_call x1, Pallas kernels, shards(): pl.pallas_call(kernel, out_shape=jax.ShapeDtypeStruct(loads.shape, F32),...  103 us

profile of v3, /device:TPU:1, one launch (start us, length us, event | category | flops | bytes accessed | tf_op | source)
XLA Modules:
  0.0 104.7 jit_solution(6453110656790466786)
XLA Ops:
  0.0 103.0 %shard_map.64 = f32[768,128]{1,0:T(8,128)} custom-call(f32[768,768]{1,0:T(8,128)} %inverse_hbm.1, f32[768,256]{1,0:T(8,128)} %basis_hbm.1, f32[2048,256]{1,0:T(8,128)} %block_hbm.1, f32[2048,256]{1,0:T(8,128)} %link_hbm.1, f32[768,128]{1,0:T(8,128)} %loads_hbm.1, s32[1,768]{1,0:T(1,128)} %order_ref.1), custom_call_target="tpu_custom_call" | custom-call | flops 4000000000 | bytes 8000000 | tf_op jit(solution)/shard_map/pallas_call | solution.py:328
  103.0 1.8 %copy.8 = f32[768,128]{1,0:T(8,128)} copy(f32[768,128]{1,0:T(8,128)} %shard_map.64) | data formatting | bytes 786432

commit v4 on v3

--- a/solution.py
+++ b/solution.py
@@ -14,7 +14,7 @@
 NRHS = 128
 LEAF = 768
 LEVELS = 8
-AHEAD = 3
+AHEAD = 2
 WIDE = RANK + NRHS
 TERMS = ((0, 0), (0, 1), (1, 0), (0, 2), (2, 0), (1, 1))
 
@@ -24,11 +24,13 @@
     return high, (x - high.astype(F32)).astype(BF)
 
 
+def dot_parts(a, b):
+    one = lambda p, q: jnp.dot(p, q, preferred_element_type=F32)
+    return one(a[0], b[0]) + (one(a[0], b[1]) + one(a[1], b[0]))
+
+
 def dot(a, b):
-    ah, al = halves(a)
-    bh, bl = halves(b)
-    one = lambda p, q: jnp.dot(p, q, preferred_element_type=F32)
-    return one(ah, bh) + (one(ah, bl) + one(al, bh))
+    return dot_parts(halves(a), halves(b))
 
 
 def dot_tn(a, b):
@@ -54,7 +56,7 @@
     return (high, mid, rest - mid)
 
 
-def rank8_product(rows, solved):
+def rank_product(rows, solved):
     a, b = parts_of(rows), parts_of(solved)
     left = jnp.concatenate([a[i] for i, _ in TERMS], axis=0).astype(BF)
     right = jnp.concatenate([b[j] for _, j in TERMS], axis=0).astype(BF)
@@ -74,9 +76,18 @@
     def column(v, j):
         return jnp.take_along_axis(v, jnp.full(tile, j, jnp.int32), axis=1)
 
+    def updated(old, first, row, columns=None):
+        columns = columns or [column(old, first + i) for i in range(8)]
+        terms = [c * r for c, r in zip(columns, row)]
+        while len(terms) > 1:
+            terms = [terms[q] + terms[q + 1] for q in range(0, len(terms), 2)]
+        here = (lane >= first) & (lane < first + 8)
+        return jnp.where(here, 0.0, old) - terms[0]
+
     near = {g: a_ref[8 * g : 8 * g + 8, :] for g in range(AHEAD + 1)}
     diag = [column(near[0], j) for j in range(8)]
     cross = [column(near[1], j) for j in range(8)]
+    lefts, rights, swept = [], [], {}
     for step in range(groups):
         first = 8 * step
         now = near.pop(step)
@@ -111,21 +122,25 @@
         solved = row[7]
         for i in range(7):
             solved = jnp.where(sub == i, row[i], solved)
-        change = rank8_product(now, solved)
+        reach = step + AHEAD + (1 - step % 2)
         later = {}
-        for g in range(step + 1, min(groups, step + AHEAD + 1)):
+        for g in range(step + 1, min(groups, reach + 1)):
             old = near[g] if g in near else a_ref[8 * g : 8 * g + 8, :]
-            columns = cross if g == step + 1 else [column(old, first + i) for i in range(8)]
-            terms = [c * r for c, r in zip(columns, row)]
-            while len(terms) > 1:
-                terms = [terms[q] + terms[q + 1] for q in range(0, len(terms), 2)]
-            later[g] = jnp.where(here, 0.0, old) - terms[0]
-        for g in range(groups):
-            rows = slice(8 * g, 8 * g + 8)
-            if g == step:
-                a_ref[rows, :] = solved
-            elif g not in later:
-                a_ref[rows, :] = jnp.where(here, 0.0, a_ref[rows, :]) - change[rows, :]
+            later[g] = updated(old, first, row, cross if g == step + 1 else None)
+        swept = {g: updated(old, first, row) for g, old in swept.items()}
+        swept[step] = solved
+        lefts.append(now)
+        rights = [jnp.where(here, 0.0, r) for r in rights] + [solved]
+        if step % 2:
+            change = rank_product(jnp.concatenate(lefts, axis=0), jnp.concatenate(rights, axis=0))
+            gone = (lane >= first - 8) & (lane < first + 8)
+            for g in range(groups):
+                rows = slice(8 * g, 8 * g + 8)
+                if g in swept:
+                    a_ref[rows, :] = swept[g]
+                elif g not in later:
+                    a_ref[rows, :] = jnp.where(gone, 0.0, a_ref[rows, :]) - change[rows, :]
+            lefts, rights, swept = [], [], {}
         near = later
         if step + 2 < groups:
             cross = [column(near[step + 2], first + 8 + i) for i in range(8)]
@@ -182,24 +197,31 @@
 
     core = lax.axis_index("dev") % 2
     mine = pl.ds(pl.multiple_of(core * HALF, HALF), HALF)
-    sides = slice(RANK, WIDE)
-
-    def exchange_half(level):
+    sides, outer = slice(RANK, WIDE), slice(HALF, RANK)
+
+    def crowded(level):
+        return (level - 5) * (level - 6) == 0
+
+    def roomy(level):
+        return (level - 5) * (level - 6) != 0
+
+
+    def exchange_half(level, columns, slot):
         return pltpu.make_async_remote_copy(
-            src_ref=lift.at[mine, sides],
-            dst_ref=received.at[level - 1, mine, sides],
-            send_sem=send_sem.at[level - 1, 3],
-            recv_sem=recv_sem.at[level - 1, 3],
+            src_ref=lift.at[mine, columns],
+            dst_ref=received.at[level - 1, mine, columns],
+            send_sem=send_sem.at[level - 1, slot],
+            recv_sem=recv_sem.at[level - 1, slot],
             device_id=partner_of(level),
             device_id_type=MESH,
         )
 
-    def relay_half(level):
+    def relay_half(level, columns, slot):
         return pltpu.make_async_remote_copy(
-            src_ref=received.at[level - 1, mine, sides],
-            dst_ref=received.at[level - 1, mine, sides],
-            send_sem=send_sem.at[level - 1, 4],
-            recv_sem=recv_sem.at[level - 1, 4],
+            src_ref=received.at[level - 1, mine, columns],
+            dst_ref=received.at[level - 1, mine, columns],
+            send_sem=send_sem.at[level - 1, slot],
+            recv_sem=recv_sem.at[level - 1, slot],
             device_id=partner_of(1),
             device_id_type=MESH,
         )
@@ -243,8 +265,18 @@
         exchange(level, 0).wait_recv()
         low[...] = block[top, 0:HALF] + joined(*PIECES[0])
         sweep(low)
-        exchange(level, 1).wait_recv()
-        exchange(level, 2).wait_recv()
+
+        @pl.when(roomy(level))
+        def _():
+            exchange(level, 1).wait_recv()
+            exchange(level, 2).wait_recv()
+
+        @pl.when(crowded(level))
+        def _():
+            exchange_half(level, outer, 1).wait_recv()
+            relay_half(level, outer, 2).start()
+            relay_half(level, outer, 2).wait()
+
         first = -low[...]
         cross = block[top, HALF:RANK] + joined(*PIECES[1])
         through = dot(first, cross)
@@ -255,41 +287,62 @@
         lifted = [
             dot_tn(link_low[:, rows], solved_low[:, columns]) for rows, columns in PIECES[:3]
         ]
+        rest_parts, turned_parts = halves(rest), halves(rest.T)
         sweep(high)
         second = -high[...]
-        for piece in range(3):
-            exchange(level, piece).wait_send()
+        exchange(level, 0).wait_send()
+
+        @pl.when(roomy(level))
+        def _():
+            exchange(level, 1).wait_send()
+            exchange(level, 2).wait_send()
+
+        @pl.when(crowded(level))
+        def _():
+            exchange_half(level, outer, 1).wait_send()
+            exchange_half(level, sides, 3).wait_recv()
+            relay_half(level, sides, 4).start()
 
         @pl.when(level < LEVELS)
         def _():
-            solved_high = dot(second, rest)
-            for piece in range(3):
-                rows, columns = PIECES[piece]
-                lift[rows, columns] = lifted[piece] + dot_tn(rest[:, rows], solved_high[:, columns])
-                exchange(level + 1, piece).start()
-            gain[slot, HALF:RANK, :] = solved_high
+            inverse_parts = halves(second)
+            near = dot_parts(inverse_parts, [p[:, :HALF] for p in rest_parts])
+            near_parts = halves(near)
+            lift[0:HALF, 0:HALF] = lifted[0] + dot_parts([p[:HALF] for p in turned_parts], near_parts)
+            exchange(level + 1, 0).start()
+            far = dot_parts(inverse_parts, [p[:, HALF:] for p in rest_parts])
+            both = dot_parts(turned_parts, halves(far))
+            lift[0:HALF, HALF:RANK] = lifted[1] + both[:HALF]
+            lift[HALF:RANK, HALF:RANK] = lifted[2] + both[HALF:]
+
+            @pl.when(roomy(level + 1))
+            def _():
+                exchange(level + 1, 1).start()
+                exchange(level + 1, 2).start()
+
+            @pl.when(crowded(level + 1))
+            def _():
+                exchange_half(level + 1, outer, 1).start()
+
+            gain[slot, HALF:RANK, 0:HALF] = near
+            gain[slot, HALF:RANK, HALF:RANK] = far
 
         pl.when(level == 1)(leaf_loads)
 
-        @pl.when(level > 1)
-        def _():
-            exchange_half(level).wait_recv()
-            relay_half(level).start()
-
         pl.when(level == 5)(to_initial_order)
 
         @pl.when(level < LEVELS)
         def _():
             gain[slot, 0:HALF, :] = solved_low - dot(through, gain[slot, HALF:RANK, :])
 
-        @pl.when(level == 1)
-        def _():
-            exchange(1, 3).wait()
-
-        @pl.when(level > 1)
-        def _():
-            relay_half(level).wait()
-            exchange_half(level).wait_send()
+        @pl.when(roomy(level))
+        def _():
+            exchange(level, 3).wait()
+
+        @pl.when(crowded(level))
+        def _():
+            relay_half(level, sides, 4).wait()
+            exchange_half(level, sides, 3).wait_send()
 
         sign = 2.0 * (level % 2).astype(F32) - 1.0
         target = sign * joined(*PIECES[3])
@@ -300,7 +353,14 @@
         @pl.when(level < LEVELS)
         def _():
             lift[:, RANK:] = dot_tn(link_low, part_low) + dot_tn(rest, part_high)
-            exchange_half(level + 1).start()
+
+            @pl.when(roomy(level + 1))
+            def _():
+                exchange(level + 1, 3).start()
+
+            @pl.when(crowded(level + 1))
+            def _():
+                exchange_half(level + 1, sides, 3).start()
 
         part[slot, 0:HALF, :] = part_low - dot(through, part_high)
         part[slot, HALF:RANK, :] = part_high

time: 105 us -> 102 us (0.971)
  Pallas kernels: 103 us -> 99.1 us
    pallas_call x1, Pallas kernels: 103 us -> 99.1 us  [shards(): pl.pallas_call(kernel, out_shape=jax.ShapeDtypeStruct(loads.shape, F32),...]
where the time goes in v4:
time: 102 us; the launch traced here: 101 us
  Pallas kernels  99.1 us (97%)
  local copies, waits for them, and re-layouts  1.77 us (2%)
    pallas_call x1, Pallas kernels, shards(): pl.pallas_call(kernel, out_shape=jax.ShapeDtypeStruct(loads.shape, F32),...  99.1 us

profile of v4, /device:TPU:1, one launch (start us, length us, event | category | flops | bytes accessed | tf_op | source)
XLA Modules:
  0.0 100.8 jit_solution(2532716118454022901)
XLA Ops:
  0.0 99.1 %shard_map.64 = f32[768,128]{1,0:T(8,128)} custom-call(f32[768,768]{1,0:T(8,128)} %inverse_hbm.1, f32[768,256]{1,0:T(8,128)} %basis_hbm.1, f32[2048,256]{1,0:T(8,128)} %block_hbm.1, f32[2048,256]{1,0:T(8,128)} %link_hbm.1, f32[768,128]{1,0:T(8,128)} %loads_hbm.1, s32[1,768]{1,0:T(1,128)} %order_ref.1), custom_call_target="tpu_custom_call" | custom-call | flops 4000000000 | bytes 8000000 | tf_op jit(solution)/shard_map/pallas_call | solution.py:388
  99.1 1.8 %copy.8 = f32[768,128]{1,0:T(8,128)} copy(f32[768,128]{1,0:T(8,128)} %shard_map.64) | data formatting | bytes 786432

commit v5 on v4

--- a/solution.py
+++ b/solution.py
@@ -15,6 +15,7 @@
 LEAF = 768
 LEVELS = 8
 AHEAD = 2
+LATE = 48
 WIDE = RANK + NRHS
 TERMS = ((0, 0), (0, 1), (1, 0), (0, 2), (2, 0), (1, 1))
 
@@ -63,7 +64,7 @@
     return lax.dot_general(left, right, (((0,), (0,)), ((), ())), preferred_element_type=F32)
 
 
-def sweep(a_ref):
+def sweep(a_ref, late=None):
     size = a_ref.shape[0]
     groups = size // 8
     tile = (8, size)
@@ -141,17 +142,21 @@
                 elif g not in later:
                     a_ref[rows, :] = jnp.where(gone, 0.0, a_ref[rows, :]) - change[rows, :]
             lefts, rights, swept = [], [], {}
+            if late is not None and first + 8 == LATE:
+                late()
         near = later
         if step + 2 < groups:
             cross = [column(near[step + 2], first + 8 + i) for i in range(8)]
 
 
 PIECES = (
-    (slice(0, 128), slice(0, 128)),
+    (slice(0, 64), slice(0, 128)),
     (slice(0, 128), slice(128, 256)),
     (slice(128, 256), slice(128, 256)),
     (slice(0, 256), slice(256, 384)),
+    (slice(64, 128), slice(0, 128)),
 )
+BLOCKS = ((slice(0, 128), slice(0, 128)),) + PIECES[1:3]
 
 
 def partner_of(level):
@@ -175,8 +180,11 @@
     in_sem, send_sem, recv_sem, out_sem,
 ):
     loaded = []
+    bands = [pl.ds(RANK * i, RANK) for i in range(LEAF // RANK)]
     for i, (src, dst) in enumerate(
-        [(basis_hbm, basis), (inverse_hbm, inverse), (loads_hbm, loads), (block_hbm, block), (link_hbm, link)]
+        [(basis_hbm, basis)]
+        + [(inverse_hbm.at[band], inverse.at[band]) for band in bands]
+        + [(loads_hbm, loads), (block_hbm, block), (link_hbm, link)]
     ):
         loaded.append(pltpu.make_async_copy(src, dst, in_sem.at[i]))
         loaded[-1].start()
@@ -227,15 +235,19 @@
         )
 
     loaded[0].wait()
-    loaded[1].wait()
-    leaf_w[...] = dot(inverse[...], basis[...])
+    basis_parts = halves(basis[...])
+    for band, copy in zip(bands, loaded[1:]):
+        copy.wait()
+        leaf_w[band, :] = dot_parts(halves(inverse[band, :]), basis_parts)
     for piece in range(3):
-        rows, columns = PIECES[piece]
+        rows, columns = BLOCKS[piece]
         lift[rows, columns] = dot_tn(basis[:, rows], leaf_w[:, columns])
         if piece == 0:
             pl.semaphore_wait(barrier, LEVELS)
         exchange(1, piece).start()
-    for copy in loaded[2:]:
+        if piece == 0:
+            exchange(1, 4).start()
+    for copy in loaded[4:]:
         copy.wait()
     rows = lax.broadcasted_iota(jnp.int32, (LEAF, LEAF), 0)
     hot[...] = jnp.where(rows == order_ref[...], 1.0, 0.0).astype(BF)
@@ -263,8 +275,18 @@
             return lift[rows, columns] + received[slot, rows, columns]
 
         exchange(level, 0).wait_recv()
-        low[...] = block[top, 0:HALF] + joined(*PIECES[0])
-        sweep(low)
+        half = HALF // 2
+        own = block[top, 0:HALF] + lift[0:HALF, 0:HALF]
+        low[0:half, :] = own[:half] + received[slot, 0:half, 0:HALF]
+        low[half:HALF, :] = own[half:]
+
+        def lower_rows():
+            exchange(level, 4).wait_recv()
+            lane = lax.broadcasted_iota(jnp.int32, (half, HALF), 1)
+            came = received[slot, half:HALF, 0:HALF]
+            low[half:HALF, :] = low[half:HALF, :] + jnp.where(lane >= LATE, came, 0.0)
+
+        sweep(low, lower_rows)
 
         @pl.when(roomy(level))
         def _():
@@ -285,12 +307,13 @@
         solved_low = dot(first, link_low)
         rest = link[bottom, :] - dot_tn(cross, solved_low)
         lifted = [
-            dot_tn(link_low[:, rows], solved_low[:, columns]) for rows, columns in PIECES[:3]
+            dot_tn(link_low[:, rows], solved_low[:, columns]) for rows, columns in BLOCKS
         ]
         rest_parts, turned_parts = halves(rest), halves(rest.T)
         sweep(high)
         second = -high[...]
         exchange(level, 0).wait_send()
+        exchange(level, 4).wait_send()
 
         @pl.when(roomy(level))
         def _():
@@ -301,7 +324,7 @@
         def _():
             exchange_half(level, outer, 1).wait_send()
             exchange_half(level, sides, 3).wait_recv()
-            relay_half(level, sides, 4).start()
+            relay_half(level, sides, 5).start()
 
         @pl.when(level < LEVELS)
         def _():
@@ -311,6 +334,7 @@
             lift[0:HALF, 0:HALF] = lifted[0] + dot_parts([p[:HALF] for p in turned_parts], near_parts)
             exchange(level + 1, 0).start()
             far = dot_parts(inverse_parts, [p[:, HALF:] for p in rest_parts])
+            exchange(level + 1, 4).start()
             both = dot_parts(turned_parts, halves(far))
             lift[0:HALF, HALF:RANK] = lifted[1] + both[:HALF]
             lift[HALF:RANK, HALF:RANK] = lifted[2] + both[HALF:]
@@ -341,7 +365,7 @@
 
         @pl.when(crowded(level))
         def _():
-            relay_half(level, sides, 4).wait()
+            relay_half(level, sides, 5).wait()
             exchange_half(level, sides, 3).wait_send()
 
         sign = 2.0 * (level % 2).astype(F32) - 1.0
@@ -407,9 +431,9 @@
             pltpu.VMEM((HALF, HALF), F32),
             pltpu.VMEM((HALF, HALF), F32),
             pltpu.VMEM((LEAF, NRHS), F32),
-            pltpu.SemaphoreType.DMA((5,)),
-            pltpu.SemaphoreType.DMA((LEVELS, 5)),
-            pltpu.SemaphoreType.DMA((LEVELS, 5)),
+            pltpu.SemaphoreType.DMA((7,)),
+            pltpu.SemaphoreType.DMA((LEVELS, 6)),
+            pltpu.SemaphoreType.DMA((LEVELS, 6)),
             pltpu.SemaphoreType.DMA,
         ],
         compiler_params=pltpu.CompilerParams(

time: 102 us -> 101 us (level)
  Pallas kernels: 99.1 us -> 98 us
where the time goes in v5:
time: 101 us; the launch traced here: 99.8 us
  Pallas kernels  98 us (97%)
  local copies, waits for them, and re-layouts  1.77 us (2%)
    pallas_call x1, Pallas kernels, shards(): pl.pallas_call(kernel, out_shape=jax.ShapeDtypeStruct(loads.shape, F32),...  98 us

profile of v5, /device:TPU:1, one launch (start us, length us, event | category | flops | bytes accessed | tf_op | source)
XLA Modules:
  0.0 99.8 jit_solution(6003609030253124191)
XLA Ops:
  0.0 98.0 %shard_map.64 = f32[768,128]{1,0:T(8,128)} custom-call(f32[768,768]{1,0:T(8,128)} %inverse_hbm.1, f32[768,256]{1,0:T(8,128)} %basis_hbm.1, f32[2048,256]{1,0:T(8,128)} %block_hbm.1, f32[2048,256]{1,0:T(8,128)} %link_hbm.1, f32[768,128]{1,0:T(8,128)} %loads_hbm.1, s32[1,768]{1,0:T(1,128)} %order_ref.1), custom_call_target="tpu_custom_call" | custom-call | flops 4000000000 | bytes 8000000 | tf_op jit(solution)/shard_map/pallas_call | solution.py:412
  98.0 1.8 %copy.8 = f32[768,128]{1,0:T(8,128)} copy(f32[768,128]{1,0:T(8,128)} %shard_map.64) | data formatting | bytes 786432

commit v6 on v5

--- a/solution.py
+++ b/solution.py
@@ -297,7 +297,7 @@
         def _():
             exchange_half(level, outer, 1).wait_recv()
             relay_half(level, outer, 2).start()
-            relay_half(level, outer, 2).wait()
+            relay_half(level, outer, 2).wait_recv()
 
         first = -low[...]
         cross = block[top, HALF:RANK] + joined(*PIECES[1])
@@ -322,6 +322,7 @@
 
         @pl.when(crowded(level))
         def _():
+            relay_half(level, outer, 2).wait_send()
             exchange_half(level, outer, 1).wait_send()
             exchange_half(level, sides, 3).wait_recv()
             relay_half(level, sides, 5).start()
@@ -361,18 +362,26 @@
 
         @pl.when(roomy(level))
         def _():
-            exchange(level, 3).wait()
+            exchange(level, 3).wait_recv()
 
         @pl.when(crowded(level))
         def _():
-            relay_half(level, sides, 5).wait()
-            exchange_half(level, sides, 3).wait_send()
+            relay_half(level, sides, 5).wait_recv()
 
         sign = 2.0 * (level % 2).astype(F32) - 1.0
         target = sign * joined(*PIECES[3])
         part_low = dot(first, target[:HALF])
         part_rest = target[HALF:] - dot_tn(cross, part_low)
         part_high = dot(second, part_rest)
+
+        @pl.when(roomy(level))
+        def _():
+            exchange(level, 3).wait_send()
+
+        @pl.when(crowded(level))
+        def _():
+            relay_half(level, sides, 5).wait_send()
+            exchange_half(level, sides, 3).wait_send()
 
         @pl.when(level < LEVELS)
         def _():

time: 101 us -> 99.8 us (0.988)
  no operation moved by 1% of the time
where the time goes in v6:
time: 99.8 us; the launch traced here: 99.1 us
  Pallas kernels  97.3 us (97%)
  local copies, waits for them, and re-layouts  1.77 us (2%)
    pallas_call x1, Pallas kernels, shards(): pl.pallas_call(kernel, out_shape=jax.ShapeDtypeStruct(loads.shape, F32),...  97.3 us

profile of v6, /device:TPU:1, one launch (start us, length us, event | category | flops | bytes accessed | tf_op | source)
XLA Modules:
  0.0 99.1 jit_solution(6161994943221590330)
XLA Ops:
  0.0 97.3 %shard_map.64 = f32[768,128]{1,0:T(8,128)} custom-call(f32[768,768]{1,0:T(8,128)} %inverse_hbm.1, f32[768,256]{1,0:T(8,128)} %basis_hbm.1, f32[2048,256]{1,0:T(8,128)} %block_hbm.1, f32[2048,256]{1,0:T(8,128)} %link_hbm.1, f32[768,128]{1,0:T(8,128)} %loads_hbm.1, s32[1,768]{1,0:T(1,128)} %order_ref.1), custom_call_target="tpu_custom_call" | custom-call | flops 4000000000 | bytes 8000000 | tf_op jit(solution)/shard_map/pallas_call | solution.py:421
  97.3 1.8 %copy.8 = f32[768,128]{1,0:T(8,128)} copy(f32[768,128]{1,0:T(8,128)} %shard_map.64) | data formatting | bytes 786432

commit v7 on v6

--- a/solution.py
+++ b/solution.py
@@ -291,7 +291,6 @@
         @pl.when(roomy(level))
         def _():
             exchange(level, 1).wait_recv()
-            exchange(level, 2).wait_recv()
 
         @pl.when(crowded(level))
         def _():
@@ -302,6 +301,11 @@
         first = -low[...]
         cross = block[top, HALF:RANK] + joined(*PIECES[1])
         through = dot(first, cross)
+
+        @pl.when(roomy(level))
+        def _():
+            exchange(level, 2).wait_recv()
+
         high[...] = block[bottom, HALF:RANK] + joined(*PIECES[2]) - dot_tn(cross, through)
         link_low = link[top, :]
         solved_low = dot(first, link_low)

time: 99.8 us -> 99.6 us (level)
  no operation moved by 1% of the time
where the time goes in v7:
time: 99.6 us; the launch traced here: 98.9 us
  Pallas kernels  97.1 us (97%)
  local copies, waits for them, and re-layouts  1.77 us (2%)
    pallas_call x1, Pallas kernels, shards(): pl.pallas_call(kernel, out_shape=jax.ShapeDtypeStruct(loads.shape, F32),...  97.1 us

profile of v7, /device:TPU:1, one launch (start us, length us, event | category | flops | bytes accessed | tf_op | source)
XLA Modules:
  0.0 98.9 jit_solution(8855531004746601681)
XLA Ops:
  0.0 97.1 %shard_map.64 = f32[768,128]{1,0:T(8,128)} custom-call(f32[768,768]{1,0:T(8,128)} %inverse_hbm.1, f32[768,256]{1,0:T(8,128)} %basis_hbm.1, f32[2048,256]{1,0:T(8,128)} %block_hbm.1, f32[2048,256]{1,0:T(8,128)} %link_hbm.1, f32[768,128]{1,0:T(8,128)} %loads_hbm.1, s32[1,768]{1,0:T(1,128)} %order_ref.1), custom_call_target="tpu_custom_call" | custom-call | flops 4000000000 | bytes 8000000 | tf_op jit(solution)/shard_map/pallas_call | solution.py:425
  97.1 1.8 %copy.8 = f32[768,128]{1,0:T(8,128)} copy(f32[768,128]{1,0:T(8,128)} %shard_map.64) | data formatting | bytes 786432
